TPU v7x, 32 devices: a whole 2x2x4 slice. The times are simulated.
32 devices in a mesh: dom: 8 (over z, y), rep: 4 (over x, core).
Axes of the slice: x: 2, y: 2, z: 4, core: 2. Of those that a mesh axis runs over, the one named last changes fastest.
Arguments:
- feats: bfloat16 [256, 32768], P('rep', 'dom'), may hold values from -6 to 6
- w_self: bfloat16 [256, 256], P(None, 'rep'), may hold values from -0.375 to 0.375
- w_neigh: bfloat16 [256, 256], P(None, 'rep'), may hold values from -3 to 3
- local_cols: int32 [256, 2], P('dom'), may hold values from 0 to 31
- local_tiles: bfloat16 [256, 2, 128, 128], P('dom'), may hold values from 0 to 3, as said below
- send_list: int32 [8, 8, 2], P('dom'), may hold values from 0 to 31
- remote_rows: int32 [8, 8, 2], P('dom'), may hold values from 0 to 31
- remote_tiles: bfloat16 [8, 8, 2, 128, 128], P('dom'), may hold values from 0 to 3, as said below
- cotangent: bfloat16 [256, 32768], P('rep', 'dom'), may hold values from -6 to 6
Outputs:
- output: bfloat16 [256, 32768], P('rep', 'dom')
- grad_feats: bfloat16 [256, 32768], P('rep', 'dom')
- grad_w_self: float32 [256, 256], P(None, 'rep')
- grad_w_neigh: float32 [256, 256], P(None, 'rep')
Inputs may be any that keep to these rules, and one draw needn't show every extreme that they name: `local_tiles`: edge weights: zero where a tile has no edge, positive otherwise. `remote_tiles`: edge weights: zero where a tile has no edge, positive otherwise.
All inputs are finite; a program needn't handle non-finite values.
Results may differ from a plain program's by a relative error of at most 0.0055.
Values may be sent and summed in bfloat16 or wider, within the bound.
A program may use at most 128 MiB of HBM per device.

v0:
```python
import jax
import jax.numpy as jnp
from jax import lax
from jax.sharding import PartitionSpec as P


def local(
    feats, w_self, w_neigh, local_cols, local_tiles, send_list, remote_rows, remote_tiles, cotangent
):
    highest = lax.Precision.HIGHEST
    feat_width, node_count = feats.shape
    blocks, local_links, tile_side, _ = local_tiles.shape
    block_ids = jnp.arange(blocks, dtype=jnp.int32)
    blocked = feats.reshape(feat_width, blocks, tile_side)
    outgoing = blocked[:, send_list[0]]
    incoming = lax.all_to_all(outgoing, "dom", split_axis=1, concat_axis=1, tiled=True)
    full_feats = lax.all_gather(feats, "rep", axis=0, tiled=True)
    gathered = blocked[:, local_cols]
    summed = jnp.einsum("fblj,blij->fbi", gathered, local_tiles, preferred_element_type=jnp.float32)
    weight_rows = jnp.sum(local_tiles, axis=(1, 3), dtype=jnp.float32)
    far_tiles = remote_tiles[0]
    far_rows = remote_rows[0]
    placing = (far_rows[:, :, None] == block_ids).astype(jnp.float32)
    far_sums = jnp.sum(far_tiles, axis=3, dtype=jnp.float32)
    divisor = 1.0 + weight_rows + jnp.einsum("ski,skb->bi", far_sums, placing, precision=highest)
    far_terms = jnp.einsum(
        "fskj,skij->fski", incoming, far_tiles, preferred_element_type=jnp.float32
    )
    summed = summed + jnp.einsum("fski,skb->fbi", far_terms, placing, precision=highest)
    aggregate = (summed / divisor).astype(jnp.bfloat16).reshape(feat_width, node_count)
    full_agg = lax.all_gather(aggregate, "rep", axis=0, tiled=True)
    preact = jnp.einsum("ab,an->bn", w_self, full_feats, preferred_element_type=jnp.float32)
    preact = preact + jnp.einsum("ab,an->bn", w_neigh, full_agg, preferred_element_type=jnp.float32)
    sigmoid_val = jax.nn.sigmoid(preact)
    output = (preact * sigmoid_val).astype(jnp.bfloat16)
    slope = sigmoid_val * (1.0 + preact * (1.0 - sigmoid_val))
    grad_pre = (cotangent.astype(jnp.float32) * slope).astype(jnp.bfloat16)
    wg_self = jnp.einsum("an,bn->ab", full_feats, grad_pre, preferred_element_type=jnp.float32)
    wg_neigh = jnp.einsum("an,bn->ab", full_agg, grad_pre, preferred_element_type=jnp.float32)
    wg_self, wg_neigh = lax.psum((wg_self, wg_neigh), "dom")
    whole_self, whole_neigh = (
        lax.all_gather(w_self, "rep", axis=1, tiled=True),
        lax.all_gather(w_neigh, "rep", axis=1, tiled=True),
    )
    offset = lax.axis_index("rep") * feat_width
    mine_self = lax.dynamic_slice_in_dim(whole_self, offset, feat_width, 0)
    mine_neigh = lax.dynamic_slice_in_dim(whole_neigh, offset, feat_width, 0)
    shard_rows = lax.all_gather(grad_pre, "rep", axis=0, tiled=True)
    back_self = jnp.dot(mine_self, shard_rows, preferred_element_type=jnp.float32)
    back_agg = jnp.dot(mine_neigh, shard_rows, preferred_element_type=jnp.float32)
    scaled = (back_agg.reshape(feat_width, blocks, tile_side) / divisor).astype(jnp.bfloat16)
    picked = scaled[:, far_rows]
    far_back = jnp.einsum("fski,skij->fskj", picked, far_tiles, preferred_element_type=jnp.float32)
    returned = lax.all_to_all(far_back, "dom", split_axis=1, concat_axis=1, tiled=True)
    near_back = jnp.einsum(
        "fbi,blij->fblj", scaled, local_tiles, preferred_element_type=jnp.float32
    )
    landing = (local_cols[:, :, None] == block_ids).astype(jnp.float32)
    collected = jnp.einsum("fblj,blc->fcj", near_back, landing, precision=highest)
    homing = (send_list[0][:, :, None] == block_ids).astype(jnp.float32)
    collected = collected + jnp.einsum("fdkj,dkc->fcj", returned, homing, precision=highest)
    grad_feats = (back_self + collected.reshape(feat_width, node_count)).astype(jnp.bfloat16)
    return (output, grad_feats, wg_self, wg_neigh)


def solution(mesh):
    placed = (
        P("rep", "dom"),
        P(None, "rep"),
        P(None, "rep"),
        P("dom", None),
        P("dom", None, None, None),
        P("dom", None, None),
        P("dom", None, None),
        P("dom", None, None, None, None),
        P("rep", "dom"),
    )
    return jax.shard_map(
        local,
        mesh=mesh,
        in_specs=placed,
        out_specs=(P("rep", "dom"), P("rep", "dom"), P(None, "rep"), P(None, "rep")),
        check_vma=False,
    )
```

profile of v0, /device:TPU:0, one launch (start us, length us, event | category | flops | bytes accessed | tf_op | source)
XLA Modules:
  0.0 199.6 jit_solution(13848253110576622706)
XLA Ops:
  7.2 0.0 copy-start.9
  7.2 0.0 copy-start.2
  7.2 0.7 compare_select_fusion.1
  7.9 0.1 copy.37
  8.0 0.1 reshape.94
  8.1 1.2 copy_bitcast_fusion.1
  9.3 0.0 copy-start
  9.3 1.3 gather_fusion.1
  10.6 7.3 %all-to-all-start = ((bf16[64,8,2,128]{3,0,2,1:T(8,128)(2,1)}), bf16[64,8,2,128]{3,0,2,1:T(8,128)(2,1)S(1)}, u32[]{:S(2)}, u32[]{:S(2)}) async-start(bf16[64,8,2,128]{3,0,2,1:T(8,128)(2,1)} %bitcast.115), calls=%async_computation | async-start | bytes 524288 | tf_op jit(solution)/shard_map/all_to_all | solution.py:16
  17.9 0.0 all-gather.6.cloned.1.call-start
  17.9 0.0 copy-done.9
  18.0 0.0 copy-done.2
  18.0 0.2 convert_reduce_fusion.1
  18.2 0.1 copy.35
  18.3 0.1 reshape.86
  18.4 0.0 copy-start.12
  18.4 1.7 gather_fusion
  20.1 0.0 copy-done
  20.1 0.6 convert_reduce_fusion
  20.7 0.0 copy-done.12
  20.7 0.3 fusion.11
  21.0 5.8 %all-to-all-done = bf16[64,8,2,128]{3,0,2,1:T(8,128)(2,1)S(1)} async-done(((bf16[64,8,2,128]{3,0,2,1:T(8,128)(2,1)}), bf16[64,8,2,128]{3,0,2,1:T(8,128)(2,1)S(1)}, u32[]{:S(2)}, u32[]{:S(2)}) %all-to-all-start) | async-done | bytes 262176 | tf_op jit(solution)/shard_map/all_to_all | solution.py:16
  26.8 0.4 convolution_bitcast_fusion.7
  27.3 0.9 convolution_bitcast_fusion.5
  28.2 1.1 fusion.10
  29.3 0.0 copy-start.7
  29.3 0.9 copy.71
  30.2 0.0 all-gather.6.cloned.1.call-update
  30.2 0.0 all-gather.4.cloned.1.call-start
  30.3 0.7 all-gather.4.cloned.1.call-update
  31.0 0.0 all-gather.8.cloned.1.call-start
  31.0 20.9 %all-gather.6.cloned.1.call-done = bf16[256,4096]{1,0:T(8,128)(2,1)} async-done(((bf16[64,4096]{1,0:T(8,128)(2,1)}), bf16[256,4096]{1,0:T(8,128)(2,1)}) %all-gather.6.cloned.1.call-update) | async-done | bytes 2097168 | tf_op jit(solution)/shard_map/all_gather | solution.py:31
  51.9 3.1 %convolution_bitcast_fusion = f32[64,4096]{1,0:T(8,128)} fusion(bf16[256,64]{0,1:T(8,128)(2,1)S(1)} %copy-done.7, bf16[256,4096]{1,0:T(8,128)(2,1)} %all-gather.6.cloned.1.call-done), kind=kOutput, calls=%fused_computation.5 | convolution fusion | flops 134217728 | bytes 3178496 | tf_op jit(solution)/shard_map/ab,an->bn/dot_general | solution.py:33
  55.0 21.1 %all-gather.4.cloned.1.call-done = bf16[256,4096]{1,0:T(8,128)(2,1)} async-done(((bf16[64,4096]{1,0:T(8,128)(2,1)}), bf16[256,4096]{1,0:T(8,128)(2,1)}) %all-gather.4.cloned.1.call-update) | async-done | bytes 2097168 | tf_op jit(solution)/shard_map/all_gather | solution.py:17
  76.1 0.0 copy-done.13
  76.1 3.6 %multiply_convert_fusion = (bf16[64,4096]{1,0:T(8,128)(2,1)}, bf16[64,4096]{1,0:T(8,128)(2,1)}) fusion(bf16[64,4096]{1,0:T(8,128)(2,1)S(1)} %copy-done.13, f32[64,4096]{1,0:T(8,128)} %convolution_bitcast_fusion, bf16[256,64]{0,1:T(8,128)(2,1)S(1)} %copy-done.8, bf16[256,4096]{1,0:T(8,128)(2,1)} %all-gather.4.cloned.1.call-done), kind=kOutput, calls=%fused_computation.28 | convolution fusion | flops 137625600 | bytes 4751360 | tf_op jit(solution)/shard_map/ab,an->bn/dot_general | solution.py:32
  79.7 0.0 all-gather.8.cloned.1.call-update
  79.7 0.1 copy.45
  79.8 0.1 reshape.102
  79.9 5.4 %all_gather.17 = bf16[256,256]{0,1:T(8,128)(2,1)S(1)} all-gather(bf16[256,64]{0,1:T(8,128)(2,1)S(1)} %copy-done.8), channel_id=1, replica_groups=mesh['dom'=8,'rep'=4] {'rep'}, dimensions={1}, use_global_device_ids=true | all-gather | bytes 163840 | tf_op jit(solution)/shard_map/all_gather | solution.py:42
  85.3 5.6 %all_gather.19 = bf16[256,256]{0,1:T(8,128)(2,1)S(1)} all-gather(bf16[256,64]{0,1:T(8,128)(2,1)S(1)} %copy-done.7), channel_id=1, replica_groups=mesh['dom'=8,'rep'=4] {'rep'}, dimensions={1}, use_global_device_ids=true | all-gather | bytes 163840 | tf_op jit(solution)/shard_map/all_gather | solution.py:43
  90.9 0.6 pad_clamp_fusion
  91.5 11.1 %all-gather.8.cloned.1.call-done = bf16[256,4096]{1,0:T(8,128)(2,1)} async-done(((bf16[64,4096]{1,0:T(8,128)(2,1)}), bf16[256,4096]{1,0:T(8,128)(2,1)}) %all-gather.8.cloned.1.call-update) | async-done | bytes 2097168 | tf_op jit(solution)/shard_map/all_gather | solution.py:48
  102.6 2.2 %convolution_bitcast_fusion.2 = f32[8,32,8,128]{3,2,1,0:T(8,128)S(1)} fusion(bf16[256,4096]{1,0:T(8,128)(2,1)} %all-gather.8.cloned.1.call-done, bf16[256,256]{0,1:T(8,128)(2,1)S(1)} %all_gather.19, s32[]{:T(128)S(6)} %select_n.29), kind=kOutput, calls=%fused_computation.12 | convolution fusion | flops 134217728 | bytes 3211268 | tf_op jit(solution)/shard_map/dot_general | solution.py:50
  104.8 0.0 copy-start.3
  104.8 0.9 fusion.12
  105.8 1.8 gather_fusion.2
  107.5 1.1 convolution_bitcast_fusion.6
  108.6 5.5 %all-to-all-start.1 = ((f32[64,8,2,128]{3,0,2,1:T(8,128)}), f32[64,8,2,128]{3,0,2,1:T(8,128)}, u32[]{:S(2)}, u32[]{:S(2)}) async-start(f32[64,8,2,128]{3,0,2,1:T(8,128)} %convolution_bitcast_fusion.6), calls=%async_computation.1 | async-start | bytes 1048576 | tf_op jit(solution)/shard_map/all_to_all | solution.py:54
  114.1 0.0 all-reduce.3.cloned.1.call-start
  114.2 3.1 %fusion.33 = f32[256,64]{0,1:T(8,128)} fusion(bf16[256,4096]{1,0:T(8,128)(2,1)} %all-gather.6.cloned.1.call-done, bf16[64,4096]{1,0:T(8,128)(2,1)S(1)} %copy-done.3), kind=kOutput, calls=%fused_computation.60 | convolution fusion | flops 134217728 | bytes 2686976 | tf_op jit(solution)/shard_map/an,bn->ab/dot_general | solution.py:39
  117.3 1.4 convolution_bitcast_fusion.8
  118.7 0.0 all-reduce.3.cloned.1.call-update
  118.7 0.0 copy-start.10
  118.8 0.4 convolution_bitcast_fusion.1
  119.2 0.2 copy-done.10
  119.4 2.1 %fusion.3 = f32[32,64,128]{2,0,1:T(8,128)S(1)} fusion(f32[64,32,2,128]{3,0,2,1:T(8,128)S(1)} %convolution_bitcast_fusion.1, s32[32,2]{0,1:T(2,128)S(1)} %copy-done.10), kind=kOutput, calls=%fused_computation.11 | convolution fusion | flops 201328640 | bytes 3145984 | tf_op jit(solution)/shard_map/fblj,blc->fcj/dot_general | solution.py:59
  121.5 0.0 copy-start.1
  121.5 8.1 %all-to-all-done.1 = f32[64,8,2,128]{3,0,2,1:T(8,128)} async-done(((f32[64,8,2,128]{3,0,2,1:T(8,128)}), f32[64,8,2,128]{3,0,2,1:T(8,128)}, u32[]{:S(2)}, u32[]{:S(2)}) %all-to-all-start.1) | async-done | bytes 524320 | tf_op jit(solution)/shard_map/all_to_all | solution.py:54
  129.6 1.9 fusion.8
  131.5 1.8 fusion
  133.3 56.8 %all-reduce.3.cloned.1.call-done = (f32[256,64]{0,1:T(8,128)}, f32[256,64]{0,1:T(8,128)}) async-done(((f32[256,64]{0,1:T(8,128)}, f32[256,64]{0,1:T(8,128)}), (f32[256,64]{0,1:T(8,128)}, f32[256,64]{0,1:T(8,128)})) %all-reduce.3.cloned.1.call-update) | async-done | bytes 131088 | tf_op jit(solution)/shard_map/psum | solution.py:40
  190.1 1.5 copy.74
  191.6 1.5 copy.75
  (18 shorter events, 0.0 us)
Async XLA Ops:
  7.2 10.8 %copy-start.9 = (s32[32,2]{0,1:T(2,128)S(1)}, s32[32,2]{0,1:T(2,128)}, u32[]{:S(2)}) copy-start(s32[32,2]{0,1:T(2,128)} %param.12) | copy-start | bytes 772
  7.2 10.8 %copy-start.2 = (bf16[1,8,2,128,128]{4,3,2,1,0:T(8,128)(2,1)S(1)}, bf16[1,8,2,128,128]{4,3,2,1,0:T(8,128)(2,1)}, u32[]{:S(2)}) copy-start(bf16[1,8,2,128,128]{4,3,2,1,0:T(8,128)(2,1)} %param.16) | copy-start | bytes 1572868
  9.3 10.8 %copy-start = (bf16[32,2,128,128]{3,2,1,0:T(8,128)(2,1)S(1)}, bf16[32,2,128,128]{3,2,1,0:T(8,128)(2,1)}, u32[]{:S(2)}) copy-start(bf16[32,2,128,128]{3,2,1,0:T(8,128)(2,1)} %param.13) | copy-start | bytes 6291460
  10.6 16.2 %all-to-all-start = ((bf16[64,8,2,128]{3,0,2,1:T(8,128)(2,1)}), bf16[64,8,2,128]{3,0,2,1:T(8,128)(2,1)S(1)}, u32[]{:S(2)}, u32[]{:S(2)}) async-start(bf16[64,8,2,128]{3,0,2,1:T(8,128)(2,1)} %bitcast.115), calls=%async_computation | async-start | bytes 524288 | tf_op jit(solution)/shard_map/all_to_all | solution.py:16
  17.9 34.1 %all-gather.6.cloned.1.call-start = ((), (), s32[]{:S(2)}) async-start(), calls=%async_computation.3 | async-start | bytes 2621440 | tf_op jit(solution)/shard_map/all_gather | solution.py:31
  18.4 2.3 %copy-start.12 = (s32[1,8,2]{1,2,0:T(2,128)S(1)}, s32[1,8,2]{1,2,0:T(2,128)}, u32[]{:S(2)}) copy-start(s32[1,8,2]{1,2,0:T(2,128)} %param.15) | copy-start | bytes 196
  26.8 1.4 copy-start.6
  29.3 22.6 %copy-start.7 = (bf16[256,64]{0,1:T(8,128)(2,1)S(1)}, bf16[256,64]{0,1:T(8,128)(2,1)}, u32[]{:S(2)}) copy-start(bf16[256,64]{0,1:T(8,128)(2,1)} %param.11) | copy-start | bytes 98308
  30.2 45.9 %copy-start.8 = (bf16[256,64]{0,1:T(8,128)(2,1)S(1)}, bf16[256,64]{0,1:T(8,128)(2,1)}, u32[]{:S(2)}) copy-start(bf16[256,64]{0,1:T(8,128)(2,1)} %param.10) | copy-start | bytes 98308
  30.2 45.9 %copy-start.13 = (bf16[64,4096]{1,0:T(8,128)(2,1)S(1)}, bf16[64,4096]{1,0:T(8,128)(2,1)}, u32[]{:S(2)}) copy-start(bf16[64,4096]{1,0:T(8,128)(2,1)} %param.17) | copy-start | bytes 1572868
  30.2 45.9 %all-gather.4.cloned.1.call-start = ((), (), s32[]{:S(2)}) async-start(), calls=%async_computation.2 | async-start | bytes 2621440 | tf_op jit(solution)/shard_map/all_gather | solution.py:17
  31.0 71.7 %all-gather.8.cloned.1.call-start = ((), (), s32[]{:S(2)}) async-start(), calls=%async_computation.4 | async-start | bytes 2621440 | tf_op jit(solution)/shard_map/all_gather | solution.py:48
  104.8 9.3 %copy-start.3 = (bf16[64,4096]{1,0:T(8,128)(2,1)S(1)}, bf16[64,4096]{1,0:T(8,128)(2,1)}, u32[]{:S(2)}) copy-start(bf16[64,4096]{1,0:T(8,128)(2,1)} %get-tuple-element.6) | copy-start | bytes 1572868
  108.6 21.0 %all-to-all-start.1 = ((f32[64,8,2,128]{3,0,2,1:T(8,128)}), f32[64,8,2,128]{3,0,2,1:T(8,128)}, u32[]{:S(2)}, u32[]{:S(2)}) async-start(f32[64,8,2,128]{3,0,2,1:T(8,128)} %convolution_bitcast_fusion.6), calls=%async_computation.1 | async-start | bytes 1048576 | tf_op jit(solution)/shard_map/all_to_all | solution.py:54
  114.1 4.6 %copy-start.4 = (bf16[64,32,128]{2,0,1:T(8,128)(2,1)S(1)}, bf16[64,32,128]{2,0,1:T(8,128)(2,1)}, u32[]{:S(2)}) copy-start(bf16[64,32,128]{2,0,1:T(8,128)(2,1)} %fusion.12) | copy-start | bytes 1572868
  114.1 76.0 %all-reduce.3.cloned.1.call-start = ((), (), s32[]{:S(2)}) async-start(), calls=%async_computation.5 | async-start | bytes 262144 | tf_op jit(solution)/shard_map/psum | solution.py:40
  114.2 3.1 %copy-start.5 = (bf16[256,4096]{1,0:T(8,128)(2,1)S(1)}, bf16[256,4096]{1,0:T(8,128)(2,1)}, u32[]{:S(2)}) copy-start(bf16[256,4096]{1,0:T(8,128)(2,1)} %all-gather.4.cloned.1.call-done) | copy-start | bytes 6291460
  118.7 0.7 copy-start.10
  119.4 10.2 %copy-start.11 = (s32[1,8,2]{1,2,0:T(2,128)S(1)}, s32[1,8,2]{1,2,0:T(2,128)}, u32[]{:S(2)}) copy-start(s32[1,8,2]{1,2,0:T(2,128)} %param.14) | copy-start | bytes 196
  121.5 10.0 %copy-start.1 = (bf16[256,4096]{1,0:T(8,128)(2,1)S(1)}, bf16[256,4096]{1,0:T(8,128)(2,1)}, u32[]{:S(2)}) copy-start(bf16[256,4096]{1,0:T(8,128)(2,1)} %all-gather.8.cloned.1.call-done) | copy-start | bytes 6291460
Sparse Core Ops, SparseCore 0:
  30.3 21.5 all-gather.5
  53.5 22.5 all-gather.3
  79.8 22.7 all-gather.7
  118.9 71.2 all-reduce.2
where the time goes:
time: 200 us
  waiting for transfers between devices  125 us (62%)
  matrix products  23.3 us (12%)
  between operations  14 us (7%)
  starting transfers between devices  13 us (6%)
  blocking collectives  11 us (6%)
  local copies, waits for them, and re-layouts  10.5 us (5%)
  other arithmetic  3.12 us (2%)
    psum x1, waiting for transfers between devices, local(): wg_self, wg_neigh = lax.psum((wg_self, wg_neigh), 'dom')  56.8 us
    all_gather x1, waiting for transfers between devices, local(): full_feats = lax.all_gather(feats, 'rep', axis=0, tiled=True)  21.1 us
    all_gather x1, waiting for transfers between devices, local(): full_agg = lax.all_gather(aggregate, 'rep', axis=0, tiled=True)  20.9 us
    all_gather x1, waiting for transfers between devices, local(): shard_rows = lax.all_gather(grad_pre, 'rep', axis=0, tiled=True)  11.1 us
    all_to_all x1, waiting for transfers between devices, local(): lax.all_to_all(far_back, 'dom', split_axis=1, concat_axis=1, tiled=True)  8.12 us
    all_to_all x1, starting transfers between devices, local(): lax.all_to_all(outgoing, 'dom', split_axis=1, concat_axis=1, tiled=True)  7.31 us
    all_to_all x1, waiting for transfers between devices, local(): lax.all_to_all(outgoing, 'dom', split_axis=1, concat_axis=1, tiled=True)  5.82 us
    all_gather x1, blocking collectives, local(): lax.all_gather(w_neigh, 'rep', axis=1, tiled=True)  5.6 us
  transfers between devices with their start and end apart: 6, of which 6 were waited for; matrix products, arithmetic and copies ran while one was open for 9% of the time, Pallas kernels for 0%

commit v1 on v0

--- a/solution.py
+++ b/solution.py
@@ -1,7 +1,26 @@
+import functools
 import jax
 import jax.numpy as jnp
 from jax import lax
 from jax.sharding import PartitionSpec as P
+
+
+def _turn_steps_all(local_values, device_axis):
+    shares = jax.lax.axis_size(device_axis)
+    local_part = local_values
+    all_blocks = [local_part]
+    later = list(map(lambda h: (h - 1, h), range(1, shares))) + [(shares - 1, 0)]
+    jj = 0
+    while jj < shares - 1:
+        local_part = jax.lax.ppermute(local_part, axis_name=device_axis, perm=later)
+        all_blocks += [local_part]
+        jj += 1
+    o_now = jnp.concatenate([*reversed(all_blocks)], 0)
+    after = jnp.roll(o_now, (jax.lax.axis_index(device_axis) + 1) * local_part.shape[0], 0)
+    return after
+
+
+body_meet = functools.partial(_turn_steps_all, device_axis="rep")
 
 
 def local(
@@ -14,7 +33,7 @@
     blocked = feats.reshape(feat_width, blocks, tile_side)
     outgoing = blocked[:, send_list[0]]
     incoming = lax.all_to_all(outgoing, "dom", split_axis=1, concat_axis=1, tiled=True)
-    full_feats = lax.all_gather(feats, "rep", axis=0, tiled=True)
+    full_feats = body_meet(feats)
     gathered = blocked[:, local_cols]
     summed = jnp.einsum("fblj,blij->fbi", gathered, local_tiles, preferred_element_type=jnp.float32)
     weight_rows = jnp.sum(local_tiles, axis=(1, 3), dtype=jnp.float32)

time: 200 us -> 182 us (0.910)
  waiting for transfers between devices: 125 us -> 92.3 us
  local copies, waits for them, and re-layouts: 10.5 us -> 23.6 us
    all_gather x1 -> x0, waiting for transfers between devices: 21.1 us -> none  [local(): full_feats = lax.all_gather(feats, 'rep', axis=0, tiled=True)]
    all_gather x1, waiting for transfers between devices: 20.9 us -> 5.85 us  [local(): full_agg = lax.all_gather(aggregate, 'rep', axis=0, tiled=True)]
    unnamed x30 -> x39, local copies, waits for them, and re-layouts: 3.23 us -> 15.4 us
    ppermute x0 -> x3, waiting for transfers between devices: none -> 10 us  [_turn_steps_all(): local_part = jax.lax.ppermute(local_part, axis_name=device_axis, perm=later)]
    all_to_all x1, waiting for transfers between devices: 5.82 us -> 0.48 us  [local(): lax.all_to_all(outgoing, 'dom', split_axis=1, concat_axis=1, tiled=True)]
  transfers between devices with their start and end apart: 6 -> 8, of which waited for: 6 -> 7; matrix products, arithmetic and copies ran while one was open for 9% -> 19% of each run, Pallas kernels for 0% -> 0%
where the time goes in v1:
time: 182 us; the launch traced here: 181 us
  waiting for transfers between devices  92.3 us (51%)
  local copies, waits for them, and re-layouts  23.6 us (13%)
  matrix products  22.1 us (12%)
  starting transfers between devices  14.6 us (8%)
  between operations  14 us (8%)
  blocking collectives  11 us (6%)
  other arithmetic  3.24 us (2%)
    psum x1, waiting for transfers between devices, local(): wg_self, wg_neigh = lax.psum((wg_self, wg_neigh), 'dom')  56.9 us
    unnamed x39, local copies, waits for them, and re-layouts  15.4 us
    all_gather x1, waiting for transfers between devices, local(): shard_rows = lax.all_gather(grad_pre, 'rep', axis=0, tiled=True)  11.2 us
    ppermute x3, waiting for transfers between devices, _turn_steps_all(): local_part = jax.lax.ppermute(local_part, axis_name=device_axis, perm=later)  10 us
    all_to_all x1, waiting for transfers between devices, local(): lax.all_to_all(far_back, 'dom', split_axis=1, concat_axis=1, tiled=True)  7.93 us
    all_to_all x1, starting transfers between devices, local(): lax.all_to_all(outgoing, 'dom', split_axis=1, concat_axis=1, tiled=True)  6.88 us
    all_gather x1, waiting for transfers between devices, local(): full_agg = lax.all_gather(aggregate, 'rep', axis=0, tiled=True)  5.85 us
    all_gather x1, blocking collectives, local(): lax.all_gather(w_self, 'rep', axis=1, tiled=True)  5.59 us
  transfers between devices with their start and end apart: 8, of which 7 were waited for; matrix products, arithmetic and copies ran while one was open for 19% of the time, Pallas kernels for 0%

profile of v1, /device:TPU:0, one launch (start us, length us, event | category | flops | bytes accessed | tf_op | source)
XLA Modules:
  0.0 180.8 jit_solution(13490284826771740564)
XLA Ops:
  7.2 0.0 copy-start.10
  7.2 0.5 collective-permute-start
  7.7 1.2 copy_bitcast_fusion.1
  8.9 0.0 copy-start
  8.9 0.8 compare_select_fusion
  9.8 0.1 copy.37
  9.9 0.1 reshape.94
  9.9 1.3 gather_fusion.1
  11.2 6.9 %all-to-all-start = ((bf16[64,8,2,128]{3,0,2,1:T(8,128)(2,1)}), bf16[64,8,2,128]{3,0,2,1:T(8,128)(2,1)S(1)}, u32[]{:S(2)}, u32[]{:S(2)}) async-start(bf16[64,8,2,128]{3,0,2,1:T(8,128)(2,1)} %bitcast.111), calls=%async_computation | async-start | bytes 524288 | tf_op jit(solution)/shard_map/all_to_all | solution.py:35
  18.1 0.0 all-gather.3.cloned.1.call-start
  18.2 0.1 copy.35
  18.3 0.1 reshape.86
  18.4 0.2 convert_reduce_fusion.1
  18.6 1.3 collective-permute-start.1
  20.0 1.7 gather_fusion
  21.7 0.6 convert_reduce_fusion
  22.3 0.3 fusion.15
  22.6 5.0 %collective-permute-done.1 = bf16[64,4096]{1,0:T(8,128)(2,1)} collective-permute-done((bf16[64,4096]{1,0:T(8,128)(2,1)}, bf16[64,4096]{1,0:T(8,128)(2,1)}, u32[]{:S(2)}, u32[]{:S(2)}) %collective-permute-start.1) | collective-permute-done | bytes 524320 | tf_op jit(solution)/shard_map/ppermute | solution.py:15
  27.6 0.5 all-to-all-done
  28.1 0.4 convolution_bitcast_fusion.6
  28.5 0.9 convolution_bitcast_fusion.4
  29.4 1.1 fusion.14
  30.6 0.9 copy.71
  31.4 0.0 all-gather.3.cloned.1.call-update
  31.5 0.0 all-gather.5.cloned.1.call-start
  31.5 5.0 %collective-permute-done.2 = bf16[64,4096]{1,0:T(8,128)(2,1)} collective-permute-done((bf16[64,4096]{1,0:T(8,128)(2,1)}, bf16[64,4096]{1,0:T(8,128)(2,1)}, u32[]{:S(2)}, u32[]{:S(2)}) %collective-permute-start.2) | collective-permute-done | bytes 524320 | tf_op jit(solution)/shard_map/ppermute | solution.py:15
  36.5 1.9 %constant_dynamic-update-slice_fusion.7 = bf16[512,4096]{1,0:T(8,128)(2,1)} fusion(bf16[64,4096]{1,0:T(8,128)(2,1)} %collective-permute-done.2), kind=kLoop, calls=%fused_computation.52 | loop fusion | bytes 1048576
  38.4 1.9 %constant_dynamic-update-slice_fusion.6 = bf16[512,4096]{1,0:T(8,128)(2,1)} fusion(bf16[512,4096]{1,0:T(8,128)(2,1)} %constant_dynamic-update-slice_fusion.7, bf16[64,4096]{1,0:T(8,128)(2,1)} %collective-permute-done.1), kind=kLoop, calls=%fused_computation.51 | loop fusion | bytes 1048576
  40.3 2.0 %constant_dynamic-update-slice_fusion.5 = bf16[512,4096]{1,0:T(8,128)(2,1)} fusion(bf16[512,4096]{1,0:T(8,128)(2,1)} %constant_dynamic-update-slice_fusion.6, bf16[64,4096]{1,0:T(8,128)(2,1)} %collective-permute-done), kind=kLoop, calls=%fused_computation.50 | loop fusion | bytes 1048576
  42.3 0.8 constant_dynamic-update-slice_fusion.4
  43.1 1.9 %constant_dynamic-update-slice_fusion.3 = bf16[512,4096]{1,0:T(8,128)(2,1)} fusion(bf16[512,4096]{1,0:T(8,128)(2,1)} %constant_dynamic-update-slice_fusion.4, bf16[64,4096]{1,0:T(8,128)(2,1)} %collective-permute-done.2), kind=kLoop, calls=%fused_computation.48 | loop fusion | bytes 1048576
  45.0 1.9 %constant_dynamic-update-slice_fusion.2 = bf16[512,4096]{1,0:T(8,128)(2,1)} fusion(bf16[512,4096]{1,0:T(8,128)(2,1)} %constant_dynamic-update-slice_fusion.3, bf16[64,4096]{1,0:T(8,128)(2,1)} %collective-permute-done.1), kind=kLoop, calls=%fused_computation.47 | loop fusion | bytes 1048576
  46.9 1.9 %constant_dynamic-update-slice_fusion.1 = bf16[512,4096]{1,0:T(8,128)(2,1)} fusion(bf16[512,4096]{1,0:T(8,128)(2,1)} %constant_dynamic-update-slice_fusion.2, bf16[64,4096]{1,0:T(8,128)(2,1)} %collective-permute-done), kind=kLoop, calls=%fused_computation.46 | loop fusion | bytes 1048576
  48.7 0.8 constant_dynamic-update-slice_fusion
  49.5 5.9 %all-gather.3.cloned.1.call-done = bf16[256,4096]{1,0:T(8,128)(2,1)} async-done(((bf16[64,4096]{1,0:T(8,128)(2,1)}), bf16[256,4096]{1,0:T(8,128)(2,1)}) %all-gather.3.cloned.1.call-update) | async-done | bytes 2097168 | tf_op jit(solution)/shard_map/all_gather | solution.py:50
  55.4 2.1 %fusion.40 = f32[4096,64]{0,1:T(8,128)S(1)} fusion(bf16[256,64]{0,1:T(8,128)(2,1)S(1)} %copy-done.8, bf16[256,4096]{1,0:T(8,128)(2,1)} %all-gather.3.cloned.1.call-done), kind=kOutput, calls=%fused_computation.73 | convolution fusion | flops 134217728 | bytes 3178496 | tf_op jit(solution)/shard_map/ab,an->bn/dot_general | solution.py:52
  57.5 3.4 %multiply_convert_fusion = (bf16[64,4096]{1,0:T(8,128)(2,1)}, bf16[64,4096]{1,0:T(8,128)(2,1)}) fusion(bf16[64,4096]{1,0:T(8,128)(2,1)S(1)} %copy-done.14, f32[4096,64]{0,1:T(8,128)S(1)} %fusion.40, bf16[256,64]{0,1:T(8,128)(2,1)S(1)} %copy-done.9, bf16[512,4096]{1,0:T(8,128)(2,1)} %constant_dynamic-update-slice_fusion, s32[]{:T(128)S(6)} %select_n.41), kind=kOutput, calls=%fused_computation.30 | convolution fusion | flops 137625600 | bytes 4751364 | tf_op jit(solution)/shard_map/ab,an->bn/dot_general | solution.py:51
  60.9 0.0 all-gather.5.cloned.1.call-update
  60.9 0.1 copy.45
  61.0 0.1 reshape.102
  61.0 5.4 %all_gather.15 = bf16[256,256]{0,1:T(8,128)(2,1)S(1)} all-gather(bf16[256,64]{0,1:T(8,128)(2,1)S(1)} %copy-done.8), channel_id=1, replica_groups=mesh['dom'=8,'rep'=4] {'rep'}, dimensions={1}, use_global_device_ids=true | all-gather | bytes 163840 | tf_op jit(solution)/shard_map/all_gather | solution.py:62
  66.4 5.6 %all_gather.13 = bf16[256,256]{0,1:T(8,128)(2,1)S(1)} all-gather(bf16[256,64]{0,1:T(8,128)(2,1)S(1)} %copy-done.9), channel_id=1, replica_groups=mesh['dom'=8,'rep'=4] {'rep'}, dimensions={1}, use_global_device_ids=true | all-gather | bytes 163840 | tf_op jit(solution)/shard_map/all_gather | solution.py:61
  72.0 0.6 pad_clamp_fusion
  72.6 11.2 %all-gather.5.cloned.1.call-done = bf16[256,4096]{1,0:T(8,128)(2,1)} async-done(((bf16[64,4096]{1,0:T(8,128)(2,1)}), bf16[256,4096]{1,0:T(8,128)(2,1)}) %all-gather.5.cloned.1.call-update) | async-done | bytes 2097168 | tf_op jit(solution)/shard_map/all_gather | solution.py:67
  83.8 2.2 %convolution_bitcast_fusion.1 = f32[8,32,8,128]{3,2,1,0:T(8,128)S(1)} fusion(bf16[256,4096]{1,0:T(8,128)(2,1)} %all-gather.5.cloned.1.call-done, bf16[256,256]{0,1:T(8,128)(2,1)S(1)} %all_gather.15, s32[]{:T(128)S(6)} %select_n.44), kind=kOutput, calls=%fused_computation.15 | convolution fusion | flops 134217728 | bytes 3211268 | tf_op jit(solution)/shard_map/dot_general | solution.py:69
  86.0 0.0 copy-start.5
  86.0 0.9 fusion.16
  86.9 1.8 gather_fusion.2
  88.7 1.1 convolution_bitcast_fusion.5
  89.7 5.5 %all-to-all-start.1 = ((f32[64,8,2,128]{3,0,2,1:T(8,128)}), f32[64,8,2,128]{3,0,2,1:T(8,128)}, u32[]{:S(2)}, u32[]{:S(2)}) async-start(f32[64,8,2,128]{3,0,2,1:T(8,128)} %convolution_bitcast_fusion.5), calls=%async_computation.1 | async-start | bytes 1048576 | tf_op jit(solution)/shard_map/all_to_all | solution.py:73
  95.3 0.2 all-reduce.3.cloned.1.call-start
  95.5 3.1 %fusion.4 = f32[256,64]{0,1:T(8,128)} fusion(bf16[64,4096]{1,0:T(8,128)(2,1)S(1)} %copy-done.5, bf16[512,4096]{1,0:T(8,128)(2,1)} %constant_dynamic-update-slice_fusion, s32[]{:T(128)S(6)} %select_n.41), kind=kOutput, calls=%fused_computation.10 | convolution fusion | flops 134217728 | bytes 2686980 | tf_op jit(solution)/shard_map/an,bn->ab/dot_general | solution.py:57
  98.7 1.4 fusion.39
  100.0 0.0 all-reduce.3.cloned.1.call-update
  100.1 0.0 copy-start.11
  100.1 0.4 convolution_bitcast_fusion
  100.5 0.2 copy-done.11
  100.8 2.1 %fusion.7 = f32[32,64,128]{2,0,1:T(8,128)S(1)} fusion(f32[64,32,2,128]{3,0,2,1:T(8,128)S(1)} %convolution_bitcast_fusion, s32[32,2]{0,1:T(2,128)S(1)} %copy-done.11), kind=kOutput, calls=%fused_computation.14 | convolution fusion | flops 201328640 | bytes 3145984 | tf_op jit(solution)/shard_map/fblj,blc->fcj/dot_general | solution.py:78
  102.8 7.9 %all-to-all-done.1 = f32[64,8,2,128]{3,0,2,1:T(8,128)} async-done(((f32[64,8,2,128]{3,0,2,1:T(8,128)}), f32[64,8,2,128]{3,0,2,1:T(8,128)}, u32[]{:S(2)}, u32[]{:S(2)}) %all-to-all-start.1) | async-done | bytes 524320 | tf_op jit(solution)/shard_map/all_to_all | solution.py:73
  110.8 1.9 %fusion.12 = f32[32,64,128]{2,0,1:T(8,128)S(1)} fusion(f32[32,64,128]{2,0,1:T(8,128)S(1)} %fusion.7, f32[64,8,2,128]{3,0,2,1:T(8,128)} %all-to-all-done.1, s32[8,2]{0,1:T(2,128)S(1)} %bitcast.112), kind=kOutput, calls=%fused_computation.21 | convolution fusion | flops 50594304 | bytes 2621504 | tf_op jit(solution)/shard_map/fdkj,dkc->fcj/dot_general | solution.py:80
  112.7 1.8 fusion.1
  114.5 56.9 %all-reduce.3.cloned.1.call-done = (f32[256,64]{0,1:T(8,128)}, f32[256,64]{0,1:T(8,128)}) async-done(((f32[256,64]{0,1:T(8,128)}, f32[256,64]{0,1:T(8,128)}), (f32[256,64]{0,1:T(8,128)}, f32[256,64]{0,1:T(8,128)})) %all-reduce.3.cloned.1.call-update) | async-done | bytes 131088 | tf_op jit(solution)/shard_map/psum | solution.py:59
  171.4 1.5 copy.81
  172.8 1.5 copy.82
  (30 shorter events, 0.1 us)
Async XLA Ops:
  7.2 11.0 %copy-start.10 = (s32[32,2]{0,1:T(2,128)S(1)}, s32[32,2]{0,1:T(2,128)}, u32[]{:S(2)}) copy-start(s32[32,2]{0,1:T(2,128)} %param.12) | copy-start | bytes 772
  7.2 11.2 %copy-start.4 = (bf16[1,8,2,128,128]{4,3,2,1,0:T(8,128)(2,1)S(1)}, bf16[1,8,2,128,128]{4,3,2,1,0:T(8,128)(2,1)}, u32[]{:S(2)}) copy-start(bf16[1,8,2,128,128]{4,3,2,1,0:T(8,128)(2,1)} %param.16) | copy-start | bytes 1572868
  7.2 11.4 %collective-permute-start = (bf16[64,4096]{1,0:T(8,128)(2,1)}, bf16[64,4096]{1,0:T(8,128)(2,1)}, u32[]{:S(2)}, u32[]{:S(2)}) collective-permute-start(bf16[64,4096]{1,0:T(8,128)(2,1)} %param.9), channel_id=1, source_target_pairs={{0,1},{1,2},{2,3},{3,0},{4,5},{5,6},{6,7},{7,4},{8,9},{9,10},{10,1... | collective-permute-start | bytes 1572872 | tf_op jit(solution)/shard_map/ppermute | solution.py:15
  8.9 12.8 %copy-start = (bf16[32,2,128,128]{3,2,1,0:T(8,128)(2,1)S(1)}, bf16[32,2,128,128]{3,2,1,0:T(8,128)(2,1)}, u32[]{:S(2)}) copy-start(bf16[32,2,128,128]{3,2,1,0:T(8,128)(2,1)} %param.13) | copy-start | bytes 6291460
  11.2 16.8 %all-to-all-start = ((bf16[64,8,2,128]{3,0,2,1:T(8,128)(2,1)}), bf16[64,8,2,128]{3,0,2,1:T(8,128)(2,1)S(1)}, u32[]{:S(2)}, u32[]{:S(2)}) async-start(bf16[64,8,2,128]{3,0,2,1:T(8,128)(2,1)} %bitcast.111), calls=%async_computation | async-start | bytes 524288 | tf_op jit(solution)/shard_map/all_to_all | solution.py:35
  18.1 37.3 %all-gather.3.cloned.1.call-start = ((), (), s32[]{:S(2)}) async-start(), calls=%async_computation.2 | async-start | bytes 2621440 | tf_op jit(solution)/shard_map/all_gather | solution.py:50
  18.6 9.0 %collective-permute-start.1 = (bf16[64,4096]{1,0:T(8,128)(2,1)}, bf16[64,4096]{1,0:T(8,128)(2,1)}, u32[]{:S(2)}, u32[]{:S(2)}) collective-permute-start(bf16[64,4096]{1,0:T(8,128)(2,1)} %collective-permute-done), channel_id=1, source_target_pairs={{0,1},{1,2},{2,3},{3,0},{4,5},{5,6},{6,7},{7,4},{8,9},{9,10},{10,1... | collective-permute-start | bytes 1572872 | tf_op jit(solution)/shard_map/ppermute | solution.py:15
  20.0 2.3 %copy-start.13 = (s32[1,8,2]{1,2,0:T(2,128)S(1)}, s32[1,8,2]{1,2,0:T(2,128)}, u32[]{:S(2)}) copy-start(s32[1,8,2]{1,2,0:T(2,128)} %param.15) | copy-start | bytes 196
  27.6 8.9 %collective-permute-start.2 = (bf16[64,4096]{1,0:T(8,128)(2,1)}, bf16[64,4096]{1,0:T(8,128)(2,1)}, u32[]{:S(2)}, u32[]{:S(2)}) collective-permute-start(bf16[64,4096]{1,0:T(8,128)(2,1)} %collective-permute-done.1), channel_id=1, source_target_pairs={{0,1},{1,2},{2,3},{3,0},{4,5},{5,6},{6,7},{7,4},{8,9},{9,10},{10,1... | collective-permute-start | bytes 1572872 | tf_op jit(solution)/shard_map/ppermute | solution.py:15
  28.1 1.4 copy-start.7
  31.4 10.8 %copy-start.3 = (bf16[64,4096]{1,0:T(8,128)(2,1)S(1)}, bf16[64,4096]{1,0:T(8,128)(2,1)}, u32[]{:S(2)}) copy-start(bf16[64,4096]{1,0:T(8,128)(2,1)} %param.9) | copy-start | bytes 1572868
  31.5 52.3 %all-gather.5.cloned.1.call-start = ((), (), s32[]{:S(2)}) async-start(), calls=%async_computation.3 | async-start | bytes 2621440 | tf_op jit(solution)/shard_map/all_gather | solution.py:67
  43.1 12.3 %copy-start.8 = (bf16[256,64]{0,1:T(8,128)(2,1)S(1)}, bf16[256,64]{0,1:T(8,128)(2,1)}, u32[]{:S(2)}) copy-start(bf16[256,64]{0,1:T(8,128)(2,1)} %param.11) | copy-start | bytes 98308
  48.7 8.7 %copy-start.9 = (bf16[256,64]{0,1:T(8,128)(2,1)S(1)}, bf16[256,64]{0,1:T(8,128)(2,1)}, u32[]{:S(2)}) copy-start(bf16[256,64]{0,1:T(8,128)(2,1)} %param.10) | copy-start | bytes 98308
  49.5 7.9 %copy-start.14 = (bf16[64,4096]{1,0:T(8,128)(2,1)S(1)}, bf16[64,4096]{1,0:T(8,128)(2,1)}, u32[]{:S(2)}) copy-start(bf16[64,4096]{1,0:T(8,128)(2,1)} %param.17) | copy-start | bytes 1572868
  86.0 9.5 %copy-start.5 = (bf16[64,4096]{1,0:T(8,128)(2,1)S(1)}, bf16[64,4096]{1,0:T(8,128)(2,1)}, u32[]{:S(2)}) copy-start(bf16[64,4096]{1,0:T(8,128)(2,1)} %get-tuple-element.6) | copy-start | bytes 1572868
  89.7 21.0 %all-to-all-start.1 = ((f32[64,8,2,128]{3,0,2,1:T(8,128)}), f32[64,8,2,128]{3,0,2,1:T(8,128)}, u32[]{:S(2)}, u32[]{:S(2)}) async-start(f32[64,8,2,128]{3,0,2,1:T(8,128)} %convolution_bitcast_fusion.5), calls=%async_computation.1 | async-start | bytes 1048576 | tf_op jit(solution)/shard_map/all_to_all | solution.py:73
  95.3 4.8 %copy-start.6 = (bf16[64,32,128]{2,0,1:T(8,128)(2,1)S(1)}, bf16[64,32,128]{2,0,1:T(8,128)(2,1)}, u32[]{:S(2)}) copy-start(bf16[64,32,128]{2,0,1:T(8,128)(2,1)} %fusion.16) | copy-start | bytes 1572868
  95.3 76.1 %all-reduce.3.cloned.1.call-start = ((), (), s32[]{:S(2)}) async-start(), calls=%async_computation.4 | async-start | bytes 262144 | tf_op jit(solution)/shard_map/psum | solution.py:59
  95.5 3.1 %copy-start.1 = (bf16[256,4096]{1,0:T(8,128)(2,1)S(1)}, bf16[256,4096]{1,0:T(8,128)(2,1)}, u32[]{:S(2)}) copy-start(bf16[256,4096]{1,0:T(8,128)(2,1)} %all-gather.3.cloned.1.call-done) | copy-start | bytes 6291460
  100.1 0.7 copy-start.11
  100.8 10.0 %copy-start.12 = (s32[1,8,2]{1,2,0:T(2,128)S(1)}, s32[1,8,2]{1,2,0:T(2,128)}, u32[]{:S(2)}) copy-start(s32[1,8,2]{1,2,0:T(2,128)} %param.14) | copy-start | bytes 196
  102.8 9.9 %copy-start.2 = (bf16[256,4096]{1,0:T(8,128)(2,1)S(1)}, bf16[256,4096]{1,0:T(8,128)(2,1)}, u32[]{:S(2)}) copy-start(bf16[256,4096]{1,0:T(8,128)(2,1)} %all-gather.5.cloned.1.call-done) | copy-start | bytes 6291460
Sparse Core Ops, SparseCore 0:
  31.6 23.7 all-gather.2
  61.0 22.7 all-gather.4
  100.2 71.1 all-reduce.2
